TPU v7x, 32 devices: a whole 2x2x4 slice. The times are simulated.
32 devices in a mesh: groups: 2 (over x), tile: 8 (over z, y), freq: 2 (over core).
Axes of the slice: x: 2, y: 2, z: 4, core: 2. Of those that a mesh axis runs over, the one named last changes fastest.
Arguments:
- panels: bfloat16 [8, 2, 256, 384], P('freq'), may hold values from -0.3125 to 0.3125
- snapshots: bfloat16 [16, 2, 32, 256], P(('groups', 'freq')), parts along dimension 0, may hold values from -6 to 6
- wavenumbers: float32 [8, 384], P('freq'), may hold values from 0.05 to 0.5
- mode_counts: int32 [8], P('freq'), may hold values from 48 to 384, as said below
- mode_mask: int32 [8, 3, 64], P('freq'), may hold values from 0 to 1, as said below
- mode_shapes: bfloat16 [8, 2048, 384], P('freq', 'tile'), may hold values from -6 to 6
Outputs:
- surface: float32 [32, 2048], P(('groups', 'tile', 'freq')), parts along dimension 0
There are 2 independent parts, one for each index of `groups`. A program takes and returns all parts, laid end to end along the dimension named above; an argument that names none is the same for every part. Nothing has to cross between parts.
Inputs may be any that keep to these rules, and one draw needn't show every extreme that they name: `mode_counts`: some frequency has exactly 384 modes and some exactly 48. `mode_mask`: mode block 0 is live in every depth block of every frequency.
All inputs are finite; a program needn't handle non-finite values.
Results may differ from a plain program's by a relative error of at most 0.0005.
Values may be sent and summed in bfloat16 or wider, within the bound.
No kernel may reach another device: no remote copies, remote signals or barrier semaphores. Data moves between devices by JAX's collectives and lax.ppermute only.
A program may use at most 64 MiB of HBM per device.

v0:
```python
import functools

import jax
import jax.numpy as jnp
from jax import lax
from jax.experimental import pallas as pl
from jax.experimental.pallas import tpu as pltpu
from jax.sharding import PartitionSpec as P

ZBLK = 32
ROWS = 16
HROWS = 32
PARTS = 4
CHUNK = 16
range_anchor = 1000.0
range_step = 25.0


def dot(a, b):
    return jnp.dot(a, b, preferred_element_type=jnp.float32)


def pieces(x):
    hi = x.astype(jnp.bfloat16).astype(jnp.float32)
    mid = (x - hi).astype(jnp.bfloat16).astype(jnp.float32)
    return hi, mid, x - hi - mid


def kernel(
    counts_hbm, shapes_hbm, panels_hbm, snaps_hbm, waves_hbm, mask_hbm, out_ref,
    counts, shapes_v, panels_v, snaps_v, waves_v, mask_v, cos_v, sin_v, row_v, col_v, live_v,
    phi_v, phib_v, gram_v, q_v, h0_v, h1_v, h2_v, w_v, level_v, energy_v, power_v, sum_v, pair_v, turn_v, sems,
    *, ranges, scale
):
    h_v = (h0_v, h1_v, h2_v)
    freqs, depths, modes = shapes_v.shape
    blocks = mask_v.shape[0]
    n = modes // blocks
    receivers = panels_v.shape[2]
    snap_count = snaps_v.shape[2]
    span = min(CHUNK, ranges)
    chunks = ranges // span
    mid = span // 2 - 1 if span > 1 else 0

    small = [
        pltpu.make_async_copy(waves_hbm, waves_v, sems.at[3, 0]),
        pltpu.make_async_copy(mask_hbm, mask_v, sems.at[4, 0]),
        pltpu.make_async_copy(counts_hbm, counts, sems.at[4, 1]),
    ]

    def loads(f):
        return [
            pltpu.make_async_copy(panels_hbm.at[f], panels_v.at[f], sems.at[0, f]),
            pltpu.make_async_copy(shapes_hbm.at[f], shapes_v.at[f], sems.at[1, f]),
            pltpu.make_async_copy(snaps_hbm.at[f], snaps_v.at[f], sems.at[2, f]),
        ]

    for copy in small:
        copy.start()
    for f in range(freqs):
        for copy in loads(f):
            copy.start()
    for copy in small:
        copy.wait()

    sum_v[...] = jnp.zeros_like(sum_v)
    waves = waves_v[...]
    angles = jnp.concatenate(
        [waves * range_step]
        + [waves * (range_anchor + range_step * (span * c + mid)) for c in range(chunks)], axis=0)
    cos_v[...] = jnp.cos(angles)
    sin_v[...] = jnp.sin(angles)
    first_block = lax.axis_index("tile") * (depths // ZBLK)
    total_blocks = mask_v.shape[2]
    pick = (
        lax.broadcasted_iota(jnp.int32, (total_blocks, depths), 0)
        == first_block + lax.broadcasted_iota(jnp.int32, (total_blocks, depths), 1) // ZBLK
    ).astype(jnp.bfloat16)
    for b in range(blocks):
        live_v[b] = dot(mask_v[b].astype(jnp.bfloat16), pick)

    def run(freq, count, nb):
        k = nb * n
        panel_re, panel_im = panels_v.at[freq, 0], panels_v.at[freq, 1]
        pairs = [(j, (j + 1) % nb if s else j) for j in range(nb) for s in range(2)]
        if nb == 1:
            pairs = [(0, 0)]
        elif nb == 2:
            pairs = [(0, 0), (0, 1), (1, 1)]
        width = [n * sum(1 for p in pairs if p[0] == j) for j in range(nb)]

        mode = lax.broadcasted_iota(jnp.int32, (n, 1), 0)
        for b in range(nb):
            part = shapes_v[freq, :, b * n:(b + 1) * n].T.astype(jnp.float32)
            part = part * live_v[b, pl.ds(freq, 1), :]
            part = jnp.where(mode + b * n < count, part, 0.0)
            phi_v[b * n:(b + 1) * n, :] = part
            phib_v[b * n:(b + 1) * n, :] = part.astype(jnp.bfloat16)
            if nb == 3 and b == 0:
                phib_v[3 * n:, :] = part.astype(jnp.bfloat16)

        snaps = jnp.concatenate([snaps_v[freq, 0], snaps_v[freq, 1]], axis=0)
        sp_re = dot(snaps, panel_re[:, :k])
        sp_im = dot(snaps, panel_im[:, :k])
        q_v[0, :, :k] = sp_re[:snap_count] + sp_im[snap_count:]
        q_v[1, :, :k] = sp_im[:snap_count] - sp_re[snap_count:]
        wide = snaps.astype(jnp.float32)
        snap_energy = jnp.maximum(jnp.sum(wide * wide, keepdims=True), 1e-30)

        eye = lax.broadcasted_iota(jnp.int32, (n, n), 0) == lax.broadcasted_iota(jnp.int32, (n, n), 1)

        def gram(p):
            j, q = pairs[p]
            left_re = panel_re[:, j * n:(j + 1) * n].T
            left_im = panel_im[:, j * n:(j + 1) * n].T
            right_re = panel_re[:, q * n:(q + 1) * n]
            right_im = panel_im[:, q * n:(q + 1) * n]
            one = dot(left_re, jnp.concatenate([right_re, right_im], axis=1))
            two = dot(left_im, jnp.concatenate([right_im, right_re], axis=1))
            g_re = one[:, :n] + two[:, :n]
            g_im = one[:, n:] - two[:, n:]
            if j == q:
                diag = jnp.sum(jnp.where(eye, g_re, 0.0), axis=1, keepdims=True)
                part = phi_v[j * n:(j + 1) * n, :]
                level_v[j:j + 1, :] = jnp.sum(part * part * diag, axis=0, keepdims=True)
                g_re = jnp.where(eye, 0.0, g_re)
                g_im = jnp.where(eye, 0.0, g_im)
            else:
                g_re, g_im = g_re * 2.0, g_im * 2.0
            gram_v[p, 0] = g_re
            gram_v[p, 1] = g_im

        def turns():
            for p, (j, q) in enumerate(pairs):
                right = jnp.concatenate([pair_v[x, :, q * n:(q + 1) * n] for x in range(5)], axis=1)
                both_of = dot(col_v[j * n:(j + 1) * n, :], right)
                for x in range(5):
                    turn_v[p, x] = both_of[:, x * n:(x + 1) * n]

        def form_q(b):
            at = slice(b * n, (b + 1) * n)
            zr, zi = q_v[0, :, at], q_v[1, :, at]
            c0, s0 = row_v[0:1, at], row_v[1:2, at]
            c1, s1 = row_v[2:3, at], row_v[3:4, at]
            turn = jnp.broadcast_to(2.0 * row_v[4:5, at], zr.shape)
            for row, low, high in (
                (0, zr * c0 - zi * s0, zr * c1 - zi * s1),
                (snap_count, zr * s0 + zi * c0, zr * s1 + zi * c1),
            ):
                a, z = low, high
                for r in range(mid, span):
                    lo = r * 2 * snap_count + row
                    w_v[lo:lo + snap_count, at] = a.astype(jnp.bfloat16)
                    if r + 1 < span:
                        a, z = z, turn * z - a
                a, z = turn * low - high, low
                for r in range(mid - 1, -1, -1):
                    lo = r * 2 * snap_count + row
                    w_v[lo:lo + snap_count, at] = a.astype(jnp.bfloat16)
                    if r:
                        a, z = turn * a - z, a

        def form_h(p, lo):
            j, q = pairs[p]
            slot = n * (p - [x[0] for x in pairs].index(j))
            g_re, g_im = gram_v[p, 0, lo:lo + HROWS, :], gram_v[p, 1, lo:lo + HROWS, :]

            cos0, sin0, cos1, sin1, turn = (
                turn_v[p, x, lo:lo + HROWS, :] for x in range(5))
            low, high = g_re * cos0 - g_im * sin0, g_re * cos1 - g_im * sin1
            h0, h1 = low, high
            for r in range(mid, span):
                h_v[j][r * n + lo:r * n + lo + HROWS, slot:slot + n] = h0.astype(jnp.bfloat16)
                if r + 1 < span:
                    h0, h1 = h1, turn * h1 - h0
            h0, h1 = turn * low - high, low
            for r in range(mid - 1, -1, -1):
                h_v[j][r * n + lo:r * n + lo + HROWS, slot:slot + n] = h0.astype(jnp.bfloat16)
                if r:
                    h0, h1 = turn * h0 - h1, h0

        step = span // PARTS if span % PARTS == 0 else span

        def power_of(c):
            y = dot(w_v[2 * snap_count * c:2 * snap_count * (c + step), :k], phib_v[:k, :])
            power_v[c:c + step] = jnp.sum((y * y).reshape(step, -1, 8, depths), axis=1)

        def energy_of(j, c):
            y = dot(h_v[j][n * c:n * (c + step), :width[j]], phib_v[j * n:j * n + width[j], :])
            y = y.reshape(step, n, depths) * phi_v[j * n:(j + 1) * n, :][None]
            y = jnp.sum(y.reshape(step, n // 8, 8, depths), axis=1)
            energy_v[c:c + step] = y if j == 0 else energy_v[c:c + step] + y

        def both(one, two):
            done = 0
            for i, task in enumerate(one):
                task()
                upto = (i + 1) * len(two) // len(one)
                for other in two[done:upto]:
                    other()
                done = upto
            for other in two[done:]:
                other()

        of = [[p for p in range(len(pairs)) if pairs[p][0] == j] for j in range(nb)]
        bind = functools.partial
        forms = [[bind(form_h, p, lo) for lo in range(0, n, HROWS) for p in of[j]] for j in range(nb)]
        grams = [[bind(gram, p) for p in of[j]] for j in range(nb)]
        starts = range(0, span, step)
        energies = [[bind(energy_of, j, c) for c in starts] for j in range(nb)]
        powers = [bind(power_of, c) for c in starts]

        for c in range(chunks):
            base = (c + 1) * freqs + freq
            cs, ss = cos_v[pl.ds(freq, 1), :], sin_v[pl.ds(freq, 1), :]
            c0, s0 = cos_v[pl.ds(base, 1), :], sin_v[pl.ds(base, 1), :]
            rows = [c0, s0, c0 * cs - s0 * ss, s0 * cs + c0 * ss, cs, ss, cs * 0.0, ss * 0.0]
            for i, row in enumerate(rows):
                row_v[i:i + 1, :] = row
            zero = jnp.zeros_like(c0)
            c1, s1 = rows[2], rows[3]
            for x, (at, one, two) in enumerate((
                (0, c0, s0), (0, s0, -c0), (2, c1, s1), (2, s1, -c1), (4, 2.0 * cs, 2.0 * ss))):
                spread = jnp.concatenate(
                    [one if i == at else two if i == at + 1 else zero for i in range(8)], axis=0)
                hi, mid_, lo = pieces(spread)
                pair_v[x] = jnp.concatenate([hi, mid_, lo, hi, mid_, hi], axis=0).astype(jnp.bfloat16)
            hi, mid_, lo = pieces(row_v[...])
            col_v[...] = jnp.concatenate([hi, hi, hi, mid_, mid_, lo], axis=0).T.astype(jnp.bfloat16)
            turns()

            first = c == 0
            if first:
                for task in grams[0]:
                    task()
            both([bind(form_q, b) for b in range(nb)], grams[1] if first and nb > 1 else [])
            both(forms[0], (grams[2] if first and nb > 2 else []) + powers)
            for j in range(1, nb):
                both(forms[j], energies[j - 1])
            for task in energies[nb - 1]:
                task()
            power = jnp.sum(power_v[...], axis=1)
            energy = jnp.sum(level_v[:nb], axis=0, keepdims=True) + jnp.sum(energy_v[...], axis=1)
            energy = jnp.maximum(energy, power / snap_energy)
            energy = energy / receivers + 1e-06
            sum_v[c * span:(c + 1) * span, :] += power * (scale / snap_count) / (
                2.0 * receivers * energy)

    @pl.loop(0, freqs)
    def _(freq):
        for copy in loads(freq):
            copy.wait()
        count = counts[0, freq]
        for b in range(1, blocks + 1):
            low = count > (b - 1) * n
            cond = jnp.logical_and(low, count <= b * n) if b < blocks else low
            pl.when(cond)(functools.partial(run, freq, count, b))

    for r in range(ranges):
        out_ref[r] = sum_v[r:r + 1, :]


def partials(panels, snapshots, wavenumbers, mode_counts, mode_mask, mode_shapes, ranges, all_freqs):
    freqs, depths, modes = mode_shapes.shape
    receivers, snap_count = panels.shape[2], snapshots.shape[2]
    blocks, total_blocks = mode_mask.shape[1], mode_mask.shape[2]
    n = modes // blocks
    span = min(CHUNK, ranges)
    trig_rows = freqs * (ranges // span + 1)
    hbm = pl.BlockSpec(memory_space=pltpu.HBM)
    f32, bf16 = jnp.float32, jnp.bfloat16
    return pl.pallas_call(
        functools.partial(kernel, ranges=ranges, scale=1.0 / all_freqs),
        out_shape=jax.ShapeDtypeStruct((ranges, 1, depths), f32),
        in_specs=[hbm] * 6,
        out_specs=pl.BlockSpec(memory_space=pltpu.VMEM),
        scratch_shapes=[
            pltpu.SMEM((1, freqs), jnp.int32),
            pltpu.VMEM((freqs, depths, modes), bf16),
            pltpu.VMEM((freqs, 2, receivers, modes), bf16),
            pltpu.VMEM((freqs, 2, snap_count, receivers), bf16),
            pltpu.VMEM((freqs, modes), f32),
            pltpu.VMEM((blocks, freqs, total_blocks), jnp.int32),
            pltpu.VMEM((trig_rows, modes), f32),
            pltpu.VMEM((trig_rows, modes), f32),
            pltpu.VMEM((8, modes), f32),
            pltpu.VMEM((modes, 48), bf16),
            pltpu.VMEM((blocks, freqs, depths), f32),
            pltpu.VMEM((modes, depths), f32),
            pltpu.VMEM((modes + n, depths), bf16),
            pltpu.VMEM((2 * blocks, 2, n, n), f32),
            pltpu.VMEM((2, snap_count, modes), f32),
            pltpu.VMEM((span * n, 2 * n), bf16),
            pltpu.VMEM((span * n, 2 * n), bf16),
            pltpu.VMEM((span * n, 2 * n), bf16),
            pltpu.VMEM((span * 2 * snap_count, modes), bf16),
            pltpu.VMEM((8, depths), f32),
            pltpu.VMEM((span, 8, depths), f32),
            pltpu.VMEM((span, 8, depths), f32),
            pltpu.VMEM((ranges, depths), f32),
            pltpu.VMEM((5, 48, modes), bf16),
            pltpu.VMEM((2 * blocks, 5, n, n), f32),
            pltpu.SemaphoreType.DMA((5, freqs)),
        ],
        compiler_params=pltpu.CompilerParams(vmem_limit_bytes=24 << 20),
        name="bartlett",
    )(*(pltpu.with_memory_space_constraint(x, pltpu.HBM) for x in (
        mode_counts.reshape(1, -1), mode_shapes, panels, snapshots, wavenumbers,
        jnp.transpose(mode_mask, (1, 0, 2)))))


def on_device(panels, snapshots, wavenumbers, mode_counts, mode_mask, mode_shapes):
    freq_count = lax.axis_size("freq")
    tile_count = lax.axis_size("tile")
    depths = mode_shapes.shape[1]
    part = partials(
        panels, snapshots, wavenumbers, mode_counts, mode_mask, mode_shapes,
        tile_count * freq_count, panels.shape[0] * freq_count,
    )
    got = lax.all_to_all(part, ("tile", "freq"), 0, 0, tiled=True)
    return jnp.sum(got.reshape(tile_count, freq_count, depths), axis=1).reshape(1, -1)


def solution(mesh):
    in_specs = (
        P("freq", None, None, None),
        P(("groups", "freq"), None, None, None),
        P("freq", None),
        P("freq"),
        P("freq", None, None),
        P("freq", "tile", None),
    )
    out_specs = P(("groups", "tile", "freq"), None)
    return jax.shard_map(
        on_device, mesh=mesh, in_specs=in_specs, out_specs=out_specs, check_vma=False
    )
```

profile of v0, /device:TPU:0, one launch (start us, length us, event | category | flops | bytes accessed | tf_op | source)
XLA Modules:
  0.0 24.5 jit_solution(18233525737732264803)
XLA Ops:
  0.0 8.2 %bartlett.1 = f32[16,1,256]{2,1,0:T(1,128)S(1)} custom-call(s32[1,4]{1,0:T(1,128)} %bitcast.7, bf16[4,256,384]{2,1,0:T(8,128)(2,1)} %shapes_hbm.1, bf16[4,2,256,384]{3,2,1,0:T(8,128)(2,1)} %panels_hbm.1, bf16[4,2,32,256]{3,2,1,0:T(8,128)(2,1)} %snaps_hbm.1, f32[4,384]{1,0:T(4,128)} %waves_hbm.1, s32[3,4,64]{2,1,0:T(4,128)} %bitcast.6), custom_call_target="tpu_custom_call" | custom-call | tf_op jit(solution)/shard_map/bartlett/pallas_call | solution.py:272
  8.3 15.5 %all_to_all.5 = f32[16,1,256]{2,1,0:T(1,128)S(1)} all-to-all(f32[16,1,256]{2,1,0:T(1,128)S(1)} %bartlett.1), channel_id=1, replica_groups=mesh['groups'=2,'tile'=8,'freq'=2] {'tile','freq'}, dimensions={0} | all-to-all | bytes 32768 | tf_op jit(solution)/shard_map/all_to_all | solution.py:320
  23.8 0.6 %copy.8 = f32[1,1,8,256]{3,1,2,0:T(1,128)} copy(f32[1,1,8,256]{3,2,1,0:T(8,128)S(1)} %bitcast.5) | data formatting | bytes 16384
  (3 shorter events, 0.1 us)
where the time goes:
time: 24.2 us; the launch traced here: 24.5 us
  blocking collectives  15.5 us (64%)
  Pallas kernels  8.25 us (34%)
  local copies, waits for them, and re-layouts  0.62 us (3%)
    all_to_all x1, blocking collectives, on_device(): got = lax.all_to_all(part, ('tile', 'freq'), 0, 0, tiled=True)  15.5 us
    pallas_call x1, Pallas kernels, partials(): pl.pallas_call(functools.partial(kernel, ranges=ranges, scale=1.0 / all_f...  8.25 us
    unnamed x1, local copies, waits for them, and re-layouts  0.61 us

commit v1 on v0

--- a/solution.py
+++ b/solution.py
@@ -10,7 +10,7 @@
 ZBLK = 32
 ROWS = 16
 HROWS = 32
-PARTS = 4
+PARTS = 2
 CHUNK = 16
 range_anchor = 1000.0
 range_step = 25.0
@@ -109,16 +109,20 @@
 
         eye = lax.broadcasted_iota(jnp.int32, (n, n), 0) == lax.broadcasted_iota(jnp.int32, (n, n), 1)
 
+        lefts = [
+            (panel_re[:, j * n:(j + 1) * n].T, panel_im[:, j * n:(j + 1) * n].T) for j in range(nb)]
+
         def gram(p):
             j, q = pairs[p]
-            left_re = panel_re[:, j * n:(j + 1) * n].T
-            left_im = panel_im[:, j * n:(j + 1) * n].T
+            left_re, left_im = lefts[j]
             right_re = panel_re[:, q * n:(q + 1) * n]
             right_im = panel_im[:, q * n:(q + 1) * n]
-            one = dot(left_re, jnp.concatenate([right_re, right_im], axis=1))
-            two = dot(left_im, jnp.concatenate([right_im, right_re], axis=1))
-            g_re = one[:, :n] + two[:, :n]
-            g_im = one[:, n:] - two[:, n:]
+            one = dot(
+                jnp.concatenate([left_re, left_im], axis=1),
+                jnp.concatenate([
+                    jnp.concatenate([right_re, right_im], axis=1),
+                    jnp.concatenate([right_im, -right_re], axis=1)], axis=0))
+            g_re, g_im = one[:, :n], one[:, n:]
             if j == q:
                 diag = jnp.sum(jnp.where(eye, g_re, 0.0), axis=1, keepdims=True)
                 part = phi_v[j * n:(j + 1) * n, :]

time: 24.2 us -> 22.9 us (0.946)
  Pallas kernels: 8.25 us -> 6.42 us
  blocking collectives: 15.5 us -> 16 us
    pallas_call x1, Pallas kernels: 8.25 us -> 6.42 us  [partials(): pl.pallas_call(functools.partial(kernel, ranges=ranges, scale=1.0 / all_f...]
    all_to_all x1, blocking collectives: 15.5 us -> 16 us  [on_device(): got = lax.all_to_all(part, ('tile', 'freq'), 0, 0, tiled=True)]
where the time goes in v1:
time: 22.9 us; the launch traced here: 23.2 us
  blocking collectives  16 us (70%)
  Pallas kernels  6.42 us (28%)
  local copies, waits for them, and re-layouts  0.62 us (3%)
    all_to_all x1, blocking collectives, on_device(): got = lax.all_to_all(part, ('tile', 'freq'), 0, 0, tiled=True)  16 us
    pallas_call x1, Pallas kernels, partials(): pl.pallas_call(functools.partial(kernel, ranges=ranges, scale=1.0 / all_f...  6.42 us
    unnamed x1, local copies, waits for them, and re-layouts  0.61 us

profile of v1, /device:TPU:0, one launch (start us, length us, event | category | flops | bytes accessed | tf_op | source)
XLA Modules:
  0.0 23.2 jit_solution(3227571839856497384)
XLA Ops:
  0.0 6.4 %bartlett.1 = f32[16,1,256]{2,1,0:T(1,128)S(1)} custom-call(s32[1,4]{1,0:T(1,128)} %bitcast.7, bf16[4,256,384]{2,1,0:T(8,128)(2,1)} %shapes_hbm.1, bf16[4,2,256,384]{3,2,1,0:T(8,128)(2,1)} %panels_hbm.1, bf16[4,2,32,256]{3,2,1,0:T(8,128)(2,1)} %snaps_hbm.1, f32[4,384]{1,0:T(4,128)} %waves_hbm.1, s32[3,4,64]{2,1,0:T(4,128)} %bitcast.6), custom_call_target="tpu_custom_call" | custom-call | tf_op jit(solution)/shard_map/bartlett/pallas_call | solution.py:276
  6.4 16.0 %all_to_all.5 = f32[16,1,256]{2,1,0:T(1,128)S(1)} all-to-all(f32[16,1,256]{2,1,0:T(1,128)S(1)} %bartlett.1), channel_id=1, replica_groups=mesh['groups'=2,'tile'=8,'freq'=2] {'tile','freq'}, dimensions={0} | all-to-all | bytes 32768 | tf_op jit(solution)/shard_map/all_to_all | solution.py:324
  22.6 0.6 %copy.8 = f32[1,1,8,256]{3,1,2,0:T(1,128)} copy(f32[1,1,8,256]{3,2,1,0:T(8,128)S(1)} %bitcast.5) | data formatting | bytes 16384
  (3 shorter events, 0.1 us)
